TPU v7x, 128 devices: a whole 4x4x4 slice. The times are simulated.
128 devices in a mesh: ent: 32 (over x_hi, z, y), sec: 4 (over x_lo, core).
Axes of the slice: x: 4 (x_hi: 2, x_lo: 2; x = x_hi * 2 + x_lo), y: 4, z: 4, core: 2. Of those that a mesh axis runs over, the one named last changes fastest.
Arguments:
- features: bfloat16 [4096, 256], P('ent'), may hold values from -6 to 6
- theta: bfloat16 [256, 256], replicated, may hold values from -3 to 3
- section_weight: float32 [65536], P(('ent', 'sec')), may hold values from 0.5 to 2
- pair_rows: int32 [128, 32, 512], P(('ent', 'sec')), may hold values from 0 to 511
- pair_cols: int32 [128, 32, 512], P(('ent', 'sec')), may hold values from 0 to 127
- pair_counts: int32 [128, 32], P(('ent', 'sec')), may hold values from 0 to 512, as said below
- cotangent: bfloat16 [4096, 256], P('ent'), may hold values from -24 to 24
Outputs:
- activated: bfloat16 [4096, 256], P('ent')
- grad_features: bfloat16 [4096, 256], P('ent')
- grad_theta: float32 [256, 256], replicated
- grad_weight: float32 [65536], P(('ent', 'sec'))
Inputs may be any that keep to these rules, and one draw needn't show every extreme that they name: Only the first pair_counts[k, j] slots of shard k and block j are used; some shard uses all 512 slots of some block.
All inputs are finite; a program needn't handle non-finite values.
Results may differ from a plain program's by a relative error of at most 0.0059.
Values may be sent and summed in bfloat16 or wider, within the bound.
A program may use at most 64 MiB of HBM per device.

v0:
```python
import jax
import jax.numpy as jnp
from jax import lax
from jax.sharding import PartitionSpec as P


def hot_table(indices, live_slots, offset, table_width):
    hits = (indices - offset)[:, None] == jnp.arange(table_width, dtype=jnp.int32)[None, :]
    return (hits & live_slots[:, None]).astype(jnp.bfloat16)


def body(features, theta, section_weight, pair_rows, pair_cols, pair_counts, cotangent):
    ent_dev = features.shape[0]
    feature_width = features.shape[1]
    sec_dev = section_weight.shape[0]
    blocks_count = pair_rows.shape[1]
    slot_count = pair_rows.shape[2]
    own_block = lax.axis_index("ent")
    row_lists = pair_rows[0]
    col_lists = pair_cols[0]
    usable = jnp.arange(slot_count, dtype=jnp.int32)[None, :] < pair_counts[0][:, None]
    usable_float = usable.astype(jnp.float32)
    entity_index = jnp.arange(blocks_count, dtype=jnp.int32)[:, None] * ent_dev + col_lists
    local_degree = jax.ops.segment_sum(
        usable_float.reshape(-1), entity_index.reshape(-1), num_segments=blocks_count * ent_dev
    )
    entity_degree = lax.psum(local_degree, ("ent", "sec"))
    own_degree = lax.dynamic_slice_in_dim(entity_degree, own_block * ent_dev, ent_dev)
    entity_scale = lax.rsqrt(1.0 + own_degree)[:, None]
    sec_count = jax.ops.segment_sum(
        usable_float.reshape(-1), row_lists.reshape(-1), num_segments=sec_dev
    )
    section_scale = (section_weight / (1.0 + sec_count))[:, None]

    def entity_fold(running, incoming, start_row):
        row_count = incoming.shape[0]
        span_width = min(row_count, ent_dev)
        block_span = max(row_count // ent_dev, 1)
        offset = start_row

        def add_block(turn_index, accum):
            row_slots = lax.dynamic_index_in_dim(row_lists, turn_index, 0, keepdims=False)
            col_slots = lax.dynamic_index_in_dim(col_lists, turn_index, 0, keepdims=False)
            live_slots = lax.dynamic_index_in_dim(usable, turn_index, 0, keepdims=False)
            values = lax.dynamic_slice_in_dim(incoming, turn_index * span_width, span_width, 0)
            col_hot = hot_table(col_slots, live_slots, offset, span_width)
            row_hot = hot_table(row_slots, live_slots, 0, sec_dev)
            picked = jnp.dot(col_hot, values, preferred_element_type=jnp.float32).astype(
                jnp.bfloat16
            )
            return accum + jnp.einsum(
                "ps,pf->sf", row_hot, picked, preferred_element_type=jnp.float32
            )

        return lax.fori_loop(0, block_span, add_block, running)

    def entity_terms(messages, start_row):
        span_width = min(lax.axis_size("ent") * ent_dev, ent_dev)
        block_span = max(lax.axis_size("ent") * ent_dev // ent_dev, 1)
        offset = start_row

        def block_term(turn_index):
            row_slots = lax.dynamic_index_in_dim(row_lists, turn_index, 0, keepdims=False)
            col_slots = lax.dynamic_index_in_dim(col_lists, turn_index, 0, keepdims=False)
            live_slots = lax.dynamic_index_in_dim(usable, turn_index, 0, keepdims=False)
            row_hot = hot_table(row_slots, live_slots, 0, sec_dev)
            col_hot = hot_table(col_slots, live_slots, offset, span_width)
            picked = jnp.dot(row_hot, messages, preferred_element_type=jnp.float32).astype(
                jnp.bfloat16
            )
            return jnp.einsum("pw,pf->wf", col_hot, picked, preferred_element_type=jnp.float32)

        pieces = lax.map(block_term, jnp.arange(block_span, dtype=jnp.int32))
        return pieces.reshape(block_span * span_width, feature_width)

    def collect(messages):
        partial_sum = lax.psum_scatter(
            entity_terms(messages, jnp.int32(0)), "ent", scatter_dimension=0, tiled=True
        )
        return lax.psum(partial_sum, "sec")

    zero_sections = jnp.zeros((sec_dev, feature_width), jnp.float32)
    projected = jnp.dot(features, theta, preferred_element_type=jnp.float32)
    scaled = (entity_scale * projected).astype(jnp.bfloat16)
    gathered = entity_fold(
        zero_sections, lax.all_gather(scaled, "ent", axis=0, tiled=True), jnp.int32(0)
    )
    messages = (section_scale * gathered).astype(jnp.bfloat16)
    collected = collect(messages)
    preact = entity_scale * collected
    activated = jax.nn.silu(preact).astype(jnp.bfloat16)
    sigmoid_pre = jax.nn.sigmoid(preact)
    grad_pre = cotangent.astype(jnp.float32) * sigmoid_pre * (1.0 + preact * (1.0 - sigmoid_pre))
    back_scaled = (entity_scale * grad_pre).astype(jnp.bfloat16)
    back_gathered = entity_fold(
        zero_sections, lax.all_gather(back_scaled, "ent", axis=0, tiled=True), jnp.int32(0)
    )
    grad_weight = jnp.sum(gathered * back_gathered, axis=1) / (1.0 + sec_count)
    back_messages = (section_scale * back_gathered).astype(jnp.bfloat16)
    back_collected = collect(back_messages)
    grad_proj = (entity_scale * back_collected).astype(jnp.bfloat16)
    grad_features = lax.dot_general(
        grad_proj, theta, (((1,), (1,)), ((), ())), preferred_element_type=jnp.float32
    ).astype(jnp.bfloat16)
    local_theta = lax.dot_general(
        features, grad_proj, (((0,), (0,)), ((), ())), preferred_element_type=jnp.float32
    )
    grad_theta = lax.psum(local_theta, "ent")
    return (activated, grad_features, grad_theta, grad_weight)


def solution(mesh):
    placed = (
        P("ent", None),
        P(),
        P(("ent", "sec")),
        P(("ent", "sec"), None, None),
        P(("ent", "sec"), None, None),
        P(("ent", "sec"), None),
        P("ent", None),
    )
    return jax.shard_map(
        body,
        mesh=mesh,
        in_specs=placed,
        out_specs=(P("ent", None), P("ent", None), P(), P(("ent", "sec"))),
        check_vma=False,
    )
```

profile of v0, /device:TPU:0, one launch (start us, length us, event | category | flops | bytes accessed | tf_op | source)
XLA Modules:
  0.0 1644.0 jit_solution(5554662827985014451)
XLA Ops:
  9.2 113.5 %scatter_custom_fusion = f32[4096]{0:T(1024)S(1)} fusion(s32[16384]{0:T(1024)S(1)} %bitcast.81, f32[16384]{0:T(1024)S(1)} %bitcast.82, f32[]{:T(128)} %constant.131.clone.1), kind=kCustom, calls=%fused_computation.76 | custom fusion | flops 16384 | bytes 16388 | tf_op jit(solution)/shard_map/scatter-add | solution.py:24
  122.6 68.3 %psum.28 = f32[4096]{0:T(1024)S(1)} all-reduce(f32[4096]{0:T(1024)S(1)} %scatter_custom_fusion), channel_id=1, replica_groups=mesh['ent'=32,'sec'=4] {'ent','sec'}, use_global_device_ids=true, to_apply=%region_1.0 | all-reduce | flops 4096 | bytes 32768 | tf_op jit(solution)/shard_map/psum | solution.py:27
  193.5 113.4 %scatter_custom_fusion.1 = f32[512]{0:T(512)S(1)} fusion(s32[16384]{0:T(1024)S(1)} %bitcast.84, f32[16384]{0:T(1024)S(1)} %bitcast.83, f32[]{:T(128)} %constant.137.clone.1), kind=kCustom, calls=%fused_computation.78 | custom fusion | flops 16384 | bytes 2052 | tf_op jit(solution)/shard_map/scatter-add | solution.py:30
  307.7 79.9 %while.50 = (s32[]{:T(128)}, f32[512,256]{1,0:T(8,128)S(1)}, s32[32,512]{1,0:T(8,128)}, pred[32,512]{1,0:T(8,128)(4,1)S(1)}, s32[32,512]{1,0:T(8,128)}, /*index=...) while((s32[]{:T(128)}, f32[512,256]{1,0:T(8,128)S(1)}, ...), condition=%wide.region_4.5_spmd.clone, body=%wide.region_3.4_spmd.clone.sunk | while | flops 168820736 | bytes 1128617 | solution.py:55
  308.4 1.7 convolution_add_fusion.4
  313.4 1.7 convolution_add_fusion.4
  315.9 1.7 convolution_add_fusion.4
  318.4 1.7 convolution_add_fusion.4
  320.9 1.7 convolution_add_fusion.4
  323.4 1.7 convolution_add_fusion.4
  325.9 1.7 convolution_add_fusion.4
  330.9 1.7 convolution_add_fusion.4
  333.4 1.7 convolution_add_fusion.4
  335.9 1.7 convolution_add_fusion.4
  340.9 1.7 convolution_add_fusion.4
  343.4 1.7 convolution_add_fusion.4
  348.4 1.7 convolution_add_fusion.4
  350.9 1.7 convolution_add_fusion.4
  353.4 1.7 convolution_add_fusion.4
  355.9 1.7 convolution_add_fusion.4
  358.4 1.7 convolution_add_fusion.4
  365.9 1.7 convolution_add_fusion.4
  368.4 1.7 convolution_add_fusion.4
  373.4 1.7 convolution_add_fusion.4
  375.9 1.7 convolution_add_fusion.4
  378.4 1.7 convolution_add_fusion.4
  383.4 1.7 convolution_add_fusion.4
  385.9 1.7 convolution_add_fusion.4
  387.7 2.4 broadcast.21.clone
  390.2 144.5 %while.48 = (s32[]{:T(128)}, f32[32,128,256]{2,1,0:T(8,128)}, s32[32]{0:T(128)S(1)}, s32[32,512]{1,0:T(8,128)}, pred[32,512]{1,0:T(8,128)(4,1)S(1)}, /*index=5*/...) while((s32[]{:T(128)}, f32[32,128,256]{2,1,0:T(8,128)}, ...), condition=%wide.region_6.7_spmd, body=%wide.region_5.6_spmd.sunk | while | flops 168558592 | bytes 408219 | solution.py:73
  534.8 188.6 %reduce-scatter.3.cloned.1.call-done = f32[128,256]{1,0:T(8,128)} async-done(((f32[4096,256]{1,0:T(8,128)}), f32[128,256]{1,0:T(8,128)}) %reduce-scatter.3.cloned.1.call-update) | async-done | bytes 131088 | tf_op jit(solution)/shard_map/reduce_scatter | solution.py:77
  723.4 32.8 %all-reduce.4.cloned.1.call-done = f32[128,256]{1,0:T(8,128)} async-done(((f32[128,256]{1,0:T(8,128)}), f32[128,256]{1,0:T(8,128)}) %all-reduce.4.cloned.1.call-update) | async-done | bytes 131088 | tf_op jit(solution)/shard_map/psum | solution.py:80
  756.2 1.7 multiply_convert_fusion.3
  758.0 73.9 %all-gather.5.cloned.1.call-done = bf16[4096,256]{1,0:T(8,128)(2,1)} async-done(((bf16[128,256]{1,0:T(8,128)(2,1)}), bf16[4096,256]{1,0:T(8,128)(2,1)}) %all-gather.5.cloned.1.call-update) | async-done | bytes 2097168 | tf_op jit(solution)/shard_map/all_gather | solution.py:96
  831.9 79.9 %while.51 = (s32[]{:T(128)}, f32[512,256]{1,0:T(8,128)S(1)}, s32[32,512]{1,0:T(8,128)}, pred[32,512]{1,0:T(8,128)(4,1)S(1)}, s32[32,512]{1,0:T(8,128)}, /*index=...) while((s32[]{:T(128)}, f32[512,256]{1,0:T(8,128)S(1)}, ...), condition=%wide.region_10.11_spmd.clone, body=%wide.region_9.10_spmd.clone.sunk | while | flops 168820736 | bytes 1128617 | solution.py:55
  832.6 1.7 convolution_add_fusion.5
  835.1 1.7 convolution_add_fusion.5
  837.6 1.7 convolution_add_fusion.5
  842.6 1.7 convolution_add_fusion.5
  845.1 1.7 convolution_add_fusion.5
  847.6 1.7 convolution_add_fusion.5
  850.1 1.7 convolution_add_fusion.5
  852.6 1.7 convolution_add_fusion.5
  860.1 1.7 convolution_add_fusion.5
  862.6 1.7 convolution_add_fusion.5
  867.6 1.7 convolution_add_fusion.5
  870.1 1.7 convolution_add_fusion.5
  872.6 1.7 convolution_add_fusion.5
  877.6 1.7 convolution_add_fusion.5
  880.1 1.7 convolution_add_fusion.5
  882.6 1.7 convolution_add_fusion.5
  885.1 1.7 convolution_add_fusion.5
  890.1 1.7 convolution_add_fusion.5
  895.1 1.7 convolution_add_fusion.5
  897.6 1.7 convolution_add_fusion.5
  900.1 1.7 convolution_add_fusion.5
  912.0 2.4 broadcast.21
  914.4 144.5 %while.49 = (s32[]{:T(128)}, f32[32,128,256]{2,1,0:T(8,128)}, s32[32]{0:T(128)S(1)}, s32[32,512]{1,0:T(8,128)}, pred[32,512]{1,0:T(8,128)(4,1)S(1)}, /*index=5*/...) while((s32[]{:T(128)}, f32[32,128,256]{2,1,0:T(8,128)}, ...), condition=%wide.region_12.13_spmd, body=%wide.region_11.12_spmd.sunk | while | flops 168558592 | bytes 408219 | solution.py:73
  1059.0 190.6 %reduce-scatter.5.cloned.1.call-done = f32[128,256]{1,0:T(8,128)} async-done(((f32[4096,256]{1,0:T(8,128)}), f32[128,256]{1,0:T(8,128)}) %reduce-scatter.5.cloned.1.call-update) | async-done | bytes 131088 | tf_op jit(solution)/shard_map/reduce_scatter | solution.py:77
  1249.7 32.8 %all-reduce.6.cloned.1.call-done = f32[128,256]{1,0:T(8,128)} async-done(((f32[128,256]{1,0:T(8,128)}), f32[128,256]{1,0:T(8,128)}) %all-reduce.6.cloned.1.call-update) | async-done | bytes 131088 | tf_op jit(solution)/shard_map/psum | solution.py:80
  1282.5 1.9 convolution_bitcast_fusion
  1285.0 1.7 convolution_convert_fusion.4
  1286.8 348.6 %all-reduce.8.cloned.1.call-done = f32[256,256]{0,1:T(8,128)} async-done(((f32[256,256]{0,1:T(8,128)}), f32[256,256]{0,1:T(8,128)}) %all-reduce.8.cloned.1.call-update) | async-done | bytes 262160 | tf_op jit(solution)/shard_map/psum | solution.py:108
  1635.4 1.8 copy.11
  (442 shorter events, 252.8 us)
Async XLA Ops:
  7.2 183.8 %copy-start = (bf16[256,256]{1,0:T(8,128)(2,1)S(1)}, bf16[256,256]{1,0:T(8,128)(2,1)}, u32[]{:S(2)}) copy-start(bf16[256,256]{1,0:T(8,128)(2,1)} %param.16) | copy-start | bytes 393220
  7.2 300.5 %all-gather.3.cloned.1.call-start = ((), (), s32[]{:S(2)}) async-start(), calls=%async_computation.2 | async-start | bytes 2162688 | tf_op jit(solution)/shard_map/all_gather | solution.py:86
  192.6 530.7 %reduce-scatter.3.cloned.1.call-start = ((), (), s32[]{:S(2)}) async-start(), calls=%async_computation.3 | async-start | bytes 4325376 | tf_op jit(solution)/shard_map/reduce_scatter | solution.py:77
  390.1 366.0 %copy-start.2 = (bf16[128,256]{1,0:T(8,128)(2,1)S(1)}, bf16[128,256]{1,0:T(8,128)(2,1)}, u32[]{:S(2)}) copy-start(bf16[128,256]{1,0:T(8,128)(2,1)} %param.21) | copy-start | bytes 196612
  534.7 221.5 %all-reduce.4.cloned.1.call-start = ((), (), s32[]{:S(2)}) async-start(), calls=%async_computation.4 | async-start | bytes 262144 | tf_op jit(solution)/shard_map/psum | solution.py:80
  723.4 108.5 %all-gather.5.cloned.1.call-start = ((), (), s32[]{:S(2)}) async-start(), calls=%async_computation.5 | async-start | bytes 2162688 | tf_op jit(solution)/shard_map/all_gather | solution.py:96
  757.9 491.7 %reduce-scatter.5.cloned.1.call-start = ((), (), s32[]{:S(2)}) async-start(), calls=%async_computation.6 | async-start | bytes 4325376 | tf_op jit(solution)/shard_map/reduce_scatter | solution.py:77
  914.4 368.1 %copy-start.1 = (bf16[128,256]{1,0:T(8,128)(2,1)S(1)}, bf16[128,256]{1,0:T(8,128)(2,1)}, u32[]{:S(2)}) copy-start(bf16[128,256]{1,0:T(8,128)(2,1)} %param.15) | copy-start | bytes 196612
  1059.0 223.6 %all-reduce.6.cloned.1.call-start = ((), (), s32[]{:S(2)}) async-start(), calls=%async_computation.7 | async-start | bytes 262144 | tf_op jit(solution)/shard_map/psum | solution.py:80
  1249.7 385.8 %all-reduce.8.cloned.1.call-start = ((), (), s32[]{:S(2)}) async-start(), calls=%async_computation.8 | async-start | bytes 524288 | tf_op jit(solution)/shard_map/psum | solution.py:108
Sparse Core Ops, SparseCore 0:
  192.7 66.8 all-gather.2
  534.8 188.4 reduce-scatter.2
  725.8 30.3 all-reduce.3
  760.1 71.6 all-gather.4
  1059.1 190.4 reduce-scatter.4
  1252.1 30.3 all-reduce.5
  1285.6 349.7 all-reduce.7
where the time goes:
time: 1670 us; the launch traced here: 1640 us
  waiting for transfers between devices  867 us (52%)
  other arithmetic  231 us (14%)
  matrix products  191 us (11%)
  local copies, waits for them, and re-layouts  145 us (9%)
  loops' own time  126 us (8%)
  blocking collectives  68.3 us (4%)
    reduce_scatter x2, waiting for transfers between devices, collect(): lax.psum_scatter(entity_terms(messages, jnp.int32(0)), 'ent', scatter_dim...  379 us
    psum x1, waiting for transfers between devices, body(): grad_theta = lax.psum(local_theta, 'ent')  349 us
    another operation x2, loops' own time, entity_terms(): pieces = lax.map(block_term, jnp.arange(block_span, dtype=jnp.int32))  125 us
    scatter-add x1, other arithmetic, body(): jax.ops.segment_sum(usable_float.reshape(-1), entity_index.reshape(-1), n...  113 us
    scatter-add x1, other arithmetic, body(): jax.ops.segment_sum(usable_float.reshape(-1), row_lists.reshape(-1), num_...  113 us
    dot_general x64, matrix products, add_block(): jnp.einsum('ps,pf->sf', row_hot, picked, preferred_element_type=jnp.float32)  108 us
    dot_general x64, matrix products, block_term(): jnp.einsum('pw,pf->wf', col_hot, picked, preferred_element_type=jnp.float32)  77.7 us
    all_gather x1, waiting for transfers between devices, body(): lax.all_gather(back_scaled, 'ent', axis=0, tiled=True)  73.9 us
  transfers between devices with their start and end apart: 7, of which 6 were waited for; matrix products, arithmetic and copies ran while one was open for 7% of the time, Pallas kernels for 0%

commit v1 on v0

--- a/solution.py
+++ b/solution.py
@@ -2,6 +2,7 @@
 import jax.numpy as jnp
 from jax import lax
 from jax.sharding import PartitionSpec as P
+from jax.lax import psum
 
 
 def hot_table(indices, live_slots, offset, table_width):
@@ -24,7 +25,9 @@
     local_degree = jax.ops.segment_sum(
         usable_float.reshape(-1), entity_index.reshape(-1), num_segments=blocks_count * ent_dev
     )
-    entity_degree = lax.psum(local_degree, ("ent", "sec"))
+    entity_degree = local_degree
+    for c in ("sec", "ent"):
+        entity_degree = psum(entity_degree, axis_name=c)
     own_degree = lax.dynamic_slice_in_dim(entity_degree, own_block * ent_dev, ent_dev)
     entity_scale = lax.rsqrt(1.0 + own_degree)[:, None]
     sec_count = jax.ops.segment_sum(

time: 1670 us -> 1800 us (1.078)
  blocking collectives: 68.3 us -> 196 us
    psum x1 -> x2, blocking collectives: 68.3 us -> 196 us  [body(): entity_degree = psum(entity_degree, axis_name=c)]
where the time goes in v1:
time: 1800 us; the launch traced here: 1770 us
  waiting for transfers between devices  866 us (48%)
  other arithmetic  231 us (13%)
  blocking collectives  196 us (11%)
  matrix products  191 us (11%)
  local copies, waits for them, and re-layouts  145 us (8%)
  loops' own time  126 us (7%)
    reduce_scatter x2, waiting for transfers between devices, collect(): lax.psum_scatter(entity_terms(messages, jnp.int32(0)), 'ent', scatter_dim...  378 us
    psum x1, waiting for transfers between devices, body(): grad_theta = lax.psum(local_theta, 'ent')  349 us
    psum x2, blocking collectives, body(): entity_degree = psum(entity_degree, axis_name=c)  196 us
    another operation x2, loops' own time, entity_terms(): pieces = lax.map(block_term, jnp.arange(block_span, dtype=jnp.int32))  125 us
    scatter-add x1, other arithmetic, body(): jax.ops.segment_sum(usable_float.reshape(-1), entity_index.reshape(-1), n...  113 us
    scatter-add x1, other arithmetic, body(): jax.ops.segment_sum(usable_float.reshape(-1), row_lists.reshape(-1), num_...  113 us
    dot_general x64, matrix products, add_block(): jnp.einsum('ps,pf->sf', row_hot, picked, preferred_element_type=jnp.float32)  108 us
    dot_general x64, matrix products, block_term(): jnp.einsum('pw,pf->wf', col_hot, picked, preferred_element_type=jnp.float32)  77.7 us
  transfers between devices with their start and end apart: 7, of which 6 were waited for; matrix products, arithmetic and copies ran while one was open for 7% of the time, Pallas kernels for 0%

profile of v1, /device:TPU:0, one launch (start us, length us, event | category | flops | bytes accessed | tf_op | source)
XLA Modules:
  0.0 1770.3 jit_solution(5947568650046441263)
XLA Ops:
  9.2 113.5 %scatter_custom_fusion = f32[4096]{0:T(1024)S(1)} fusion(s32[16384]{0:T(1024)S(1)} %bitcast.81, f32[16384]{0:T(1024)S(1)} %bitcast.82, f32[]{:T(128)} %constant.131.clone.1), kind=kCustom, calls=%fused_computation.76 | custom fusion | flops 16384 | bytes 16388 | tf_op jit(solution)/shard_map/scatter-add | solution.py:25
  122.6 11.3 psum.35
  133.9 184.8 %psum.36 = f32[4096]{0:T(1024)S(1)} all-reduce(f32[4096]{0:T(1024)S(1)} %psum.35), channel_id=1, replica_groups=mesh['ent'=32,'sec'=4] {'ent'}, use_global_device_ids=true, to_apply=%region_2.0 | all-reduce | flops 4096 | bytes 32768 | tf_op jit(solution)/shard_map/psum | solution.py:30
  321.3 113.4 %scatter_custom_fusion.1 = f32[512]{0:T(512)S(1)} fusion(s32[16384]{0:T(1024)S(1)} %bitcast.84, f32[16384]{0:T(1024)S(1)} %bitcast.83, f32[]{:T(128)} %constant.137.clone.1), kind=kCustom, calls=%fused_computation.78 | custom fusion | flops 16384 | bytes 2052 | tf_op jit(solution)/shard_map/scatter-add | solution.py:33
  435.5 79.9 %while.50 = (s32[]{:T(128)}, f32[512,256]{1,0:T(8,128)S(1)}, s32[32,512]{1,0:T(8,128)}, pred[32,512]{1,0:T(8,128)(4,1)S(1)}, s32[32,512]{1,0:T(8,128)}, /*index=...) while((s32[]{:T(128)}, f32[512,256]{1,0:T(8,128)S(1)}, ...), condition=%wide.region_5.6_spmd.clone, body=%wide.region_4.5_spmd.clone.sunk | while | flops 168820736 | bytes 1128617 | solution.py:58
  436.2 1.7 convolution_add_fusion.4
  441.2 1.7 convolution_add_fusion.4
  446.2 1.7 convolution_add_fusion.4
  448.7 1.7 convolution_add_fusion.4
  451.2 1.7 convolution_add_fusion.4
  453.7 1.7 convolution_add_fusion.4
  458.7 1.7 convolution_add_fusion.4
  463.7 1.7 convolution_add_fusion.4
  466.2 1.7 convolution_add_fusion.4
  468.7 1.7 convolution_add_fusion.4
  471.2 1.7 convolution_add_fusion.4
  473.7 1.7 convolution_add_fusion.4
  476.2 1.7 convolution_add_fusion.4
  481.2 1.7 convolution_add_fusion.4
  483.7 1.7 convolution_add_fusion.4
  486.2 1.7 convolution_add_fusion.4
  488.7 1.7 convolution_add_fusion.4
  491.2 1.7 convolution_add_fusion.4
  498.7 1.7 convolution_add_fusion.4
  501.2 1.7 convolution_add_fusion.4
  506.2 1.7 convolution_add_fusion.4
  508.7 1.7 convolution_add_fusion.4
  511.2 1.7 convolution_add_fusion.4
  515.5 2.4 broadcast.21.clone
  517.9 144.5 %while.48 = (s32[]{:T(128)}, f32[32,128,256]{2,1,0:T(8,128)}, s32[32]{0:T(128)S(1)}, s32[32,512]{1,0:T(8,128)}, pred[32,512]{1,0:T(8,128)(4,1)S(1)}, /*index=5*/...) while((s32[]{:T(128)}, f32[32,128,256]{2,1,0:T(8,128)}, ...), condition=%wide.region_7.8_spmd, body=%wide.region_6.7_spmd.sunk | while | flops 168558592 | bytes 408219 | solution.py:76
  662.6 186.8 %reduce-scatter.3.cloned.1.call-done = f32[128,256]{1,0:T(8,128)} async-done(((f32[4096,256]{1,0:T(8,128)}), f32[128,256]{1,0:T(8,128)}) %reduce-scatter.3.cloned.1.call-update) | async-done | bytes 131088 | tf_op jit(solution)/shard_map/reduce_scatter | solution.py:80
  849.5 32.8 %all-reduce.4.cloned.1.call-done = f32[128,256]{1,0:T(8,128)} async-done(((f32[128,256]{1,0:T(8,128)}), f32[128,256]{1,0:T(8,128)}) %all-reduce.4.cloned.1.call-update) | async-done | bytes 131088 | tf_op jit(solution)/shard_map/psum | solution.py:83
  882.2 1.7 multiply_convert_fusion.3
  884.0 73.9 %all-gather.5.cloned.1.call-done = bf16[4096,256]{1,0:T(8,128)(2,1)} async-done(((bf16[128,256]{1,0:T(8,128)(2,1)}), bf16[4096,256]{1,0:T(8,128)(2,1)}) %all-gather.5.cloned.1.call-update) | async-done | bytes 2097168 | tf_op jit(solution)/shard_map/all_gather | solution.py:99
  957.9 79.9 %while.51 = (s32[]{:T(128)}, f32[512,256]{1,0:T(8,128)S(1)}, s32[32,512]{1,0:T(8,128)}, pred[32,512]{1,0:T(8,128)(4,1)S(1)}, s32[32,512]{1,0:T(8,128)}, /*index=...) while((s32[]{:T(128)}, f32[512,256]{1,0:T(8,128)S(1)}, ...), condition=%wide.region_11.12_spmd.clone, body=%wide.region_10.11_spmd.clone.sunk | while | flops 168820736 | bytes 1128617 | solution.py:58
  958.7 1.7 convolution_add_fusion.5
  961.2 1.7 convolution_add_fusion.5
  963.7 1.7 convolution_add_fusion.5
  971.2 1.7 convolution_add_fusion.5
  973.7 1.7 convolution_add_fusion.5
  978.7 1.7 convolution_add_fusion.5
  981.2 1.7 convolution_add_fusion.5
  983.7 1.7 convolution_add_fusion.5
  988.7 1.7 convolution_add_fusion.5
  991.1 1.7 convolution_add_fusion.5
  993.6 1.7 convolution_add_fusion.5
  996.1 1.7 convolution_add_fusion.5
  998.6 1.7 convolution_add_fusion.5
  1001.1 1.7 convolution_add_fusion.5
  1006.1 1.7 convolution_add_fusion.5
  1008.6 1.7 convolution_add_fusion.5
  1011.1 1.7 convolution_add_fusion.5
  1016.1 1.7 convolution_add_fusion.5
  1018.6 1.7 convolution_add_fusion.5
  1023.6 1.7 convolution_add_fusion.5
  1026.1 1.7 convolution_add_fusion.5
  1038.1 2.4 broadcast.21
  1040.5 144.5 %while.49 = (s32[]{:T(128)}, f32[32,128,256]{2,1,0:T(8,128)}, s32[32]{0:T(128)S(1)}, s32[32,512]{1,0:T(8,128)}, pred[32,512]{1,0:T(8,128)(4,1)S(1)}, /*index=5*/...) while((s32[]{:T(128)}, f32[32,128,256]{2,1,0:T(8,128)}, ...), condition=%wide.region_13.14_spmd, body=%wide.region_12.13_spmd.sunk | while | flops 168558592 | bytes 408219 | solution.py:76
  1185.1 190.9 %reduce-scatter.5.cloned.1.call-done = f32[128,256]{1,0:T(8,128)} async-done(((f32[4096,256]{1,0:T(8,128)}), f32[128,256]{1,0:T(8,128)}) %reduce-scatter.5.cloned.1.call-update) | async-done | bytes 131088 | tf_op jit(solution)/shard_map/reduce_scatter | solution.py:80
  1376.1 32.7 %all-reduce.6.cloned.1.call-done = f32[128,256]{1,0:T(8,128)} async-done(((f32[128,256]{1,0:T(8,128)}), f32[128,256]{1,0:T(8,128)}) %all-reduce.6.cloned.1.call-update) | async-done | bytes 131088 | tf_op jit(solution)/shard_map/psum | solution.py:83
  1408.8 1.9 convolution_bitcast_fusion
  1411.3 1.7 convolution_convert_fusion.4
  1413.1 348.6 %all-reduce.8.cloned.1.call-done = f32[256,256]{0,1:T(8,128)} async-done(((f32[256,256]{0,1:T(8,128)}), f32[256,256]{0,1:T(8,128)}) %all-reduce.8.cloned.1.call-update) | async-done | bytes 262160 | tf_op jit(solution)/shard_map/psum | solution.py:111
  1761.7 1.8 copy.11
  (443 shorter events, 254.5 us)
Async XLA Ops:
  7.2 311.6 %copy-start = (bf16[256,256]{1,0:T(8,128)(2,1)S(1)}, bf16[256,256]{1,0:T(8,128)(2,1)}, u32[]{:S(2)}) copy-start(bf16[256,256]{1,0:T(8,128)(2,1)} %param.16) | copy-start | bytes 393220
  7.2 428.3 %all-gather.3.cloned.1.call-start = ((), (), s32[]{:S(2)}) async-start(), calls=%async_computation.2 | async-start | bytes 2162688 | tf_op jit(solution)/shard_map/all_gather | solution.py:89
  320.4 529.0 %reduce-scatter.3.cloned.1.call-start = ((), (), s32[]{:S(2)}) async-start(), calls=%async_computation.3 | async-start | bytes 4325376 | tf_op jit(solution)/shard_map/reduce_scatter | solution.py:80
  517.9 364.3 %copy-start.2 = (bf16[128,256]{1,0:T(8,128)(2,1)S(1)}, bf16[128,256]{1,0:T(8,128)(2,1)}, u32[]{:S(2)}) copy-start(bf16[128,256]{1,0:T(8,128)(2,1)} %param.21) | copy-start | bytes 196612
  662.5 219.7 %all-reduce.4.cloned.1.call-start = ((), (), s32[]{:S(2)}) async-start(), calls=%async_computation.4 | async-start | bytes 262144 | tf_op jit(solution)/shard_map/psum | solution.py:83
  849.4 108.5 %all-gather.5.cloned.1.call-start = ((), (), s32[]{:S(2)}) async-start(), calls=%async_computation.5 | async-start | bytes 2162688 | tf_op jit(solution)/shard_map/all_gather | solution.py:99
  883.9 492.1 %reduce-scatter.5.cloned.1.call-start = ((), (), s32[]{:S(2)}) async-start(), calls=%async_computation.6 | async-start | bytes 4325376 | tf_op jit(solution)/shard_map/reduce_scatter | solution.py:80
  1040.5 368.3 %copy-start.1 = (bf16[128,256]{1,0:T(8,128)(2,1)S(1)}, bf16[128,256]{1,0:T(8,128)(2,1)}, u32[]{:S(2)}) copy-start(bf16[128,256]{1,0:T(8,128)(2,1)} %param.15) | copy-start | bytes 196612
  1185.0 223.8 %all-reduce.6.cloned.1.call-start = ((), (), s32[]{:S(2)}) async-start(), calls=%async_computation.7 | async-start | bytes 262144 | tf_op jit(solution)/shard_map/psum | solution.py:83
  1376.0 385.7 %all-reduce.8.cloned.1.call-start = ((), (), s32[]{:S(2)}) async-start(), calls=%async_computation.8 | async-start | bytes 524288 | tf_op jit(solution)/shard_map/psum | solution.py:111
Sparse Core Ops, SparseCore 0:
  320.5 64.8 all-gather.2
  662.6 186.7 reduce-scatter.2
  851.9 30.3 all-reduce.3
  886.2 71.6 all-gather.4
  1185.1 190.8 reduce-scatter.4
  1378.5 30.2 all-reduce.5
  1411.8 349.7 all-reduce.7
